TPU v7x, 32 devices: a whole 2x2x4 slice. The times are simulated.
32 devices in a mesh: gx: 4 (over z), gy: 4 (over y, core), gz: 2 (over x).
Axes of the slice: x: 2, y: 2, z: 4, core: 2. Of those that a mesh axis runs over, the one named last changes fastest.
Arguments:
- node_irreps: bfloat16 [4, 4, 2, 16, 25, 128], P('gx', 'gy', 'gz'), may hold values from -5 to 11
- positions: float32 [4, 4, 2, 3, 16], P('gx', 'gy', 'gz'), may hold values from 0 to 6.8
- send_list: int32 [4, 4, 2, 8], P('gx', 'gy', 'gz'), may hold values from 0 to 15, as said below
- neighbours: int32 [4, 4, 2, 16, 32], P('gx', 'gy', 'gz'), may hold values from 0 to 231
- displacements: float32 [4, 4, 2, 3, 512], P('gx', 'gy', 'gz'), may hold values from -6 to 6
- order_zero: bfloat16 [640, 640], replicated, may hold values from -0.25 to 0.25
- order_one: bfloat16 [512, 1024], replicated, may hold values from -0.25 to 0.25
- order_two: bfloat16 [384, 768], replicated, may hold values from -0.3125 to 0.3125
- reciprocal_triples: int32 [1024, 3], replicated, may hold values from -6 to 6
- reciprocal_filter: float32 [1024, 128], replicated, may hold values from 0.1 to 1
- cotangent: float32 [4, 4, 2, 16, 128], P('gx', 'gy', 'gz'), may hold values from -5 to 11
Outputs:
- updated: bfloat16 [4, 4, 2, 16, 25, 128], P('gx', 'gy', 'gz')
- long_range: float32 [4, 4, 2, 16, 128], P('gx', 'gy', 'gz')
- charge_grad: float32 [4, 4, 2, 16, 128], P('gx', 'gy', 'gz')
- position_grad: float32 [4, 4, 2, 3, 16], P('gx', 'gy', 'gz')
Inputs may be any that keep to these rules, and one draw needn't show every extreme that they name: `send_list`: entries of one block are distinct atoms of that block.
All inputs are finite; a program needn't handle non-finite values.
Results may differ from a plain program's by a relative error of at most 0.0023.
Values may be sent and summed in bfloat16 or wider, within the bound.
No kernel may reach another device: no remote copies, remote signals or barrier semaphores. Data moves between devices by JAX's collectives and lax.ppermute only.
A program may use at most 64 MiB of HBM per device.

v0:
```python
import math
import jax
import jax.numpy as jnp
from jax import lax
from jax.sharding import PartitionSpec as P

highest = lax.Precision.HIGHEST
cell_length = 6.8
planar_floor = 0.25
radial_width = 64.0


def with_halo(block, sides, width):
    for axis, dim in sides:
        count = lax.axis_size(axis)
        forward = [(i, i + 1) for i in range(count - 1)]
        forward.append((count - 1, 0))
        backward = [(target, source) for source, target in forward]
        low = lax.ppermute(
            lax.slice_in_dim(block, block.shape[dim] - width, None, axis=dim), axis, forward
        )
        high = lax.ppermute(lax.slice_in_dim(block, 0, width, axis=dim), axis, backward)
        block = jnp.concatenate([low, block, high], axis=dim)
    return block


def harmonic_slot(degree, signed_order):
    return degree * degree + degree + signed_order


def kept_rows():
    layout = []
    for degree in range(5):
        for signed_order in range(-degree, degree + 1):
            layout.append(harmonic_slot(degree, signed_order))
    return layout


def edge_messages(
    lookup_table, displacement, neighbour_index, order_zero, order_one, order_two, layout
):
    atom_count = neighbour_index.shape[0]
    neighbour_count = neighbour_index.shape[1]
    flat_index = neighbour_index.reshape(-1)
    edge_count = flat_index.shape[0]
    feature_width = lookup_table.shape[2]
    source = lookup_table[flat_index]
    length_squared = jnp.sum(displacement * displacement, axis=0)
    radial = jnp.exp(-length_squared / radial_width) / math.sqrt(neighbour_count)
    planar = jnp.sqrt(
        displacement[0] * displacement[0] + displacement[1] * displacement[1] + planar_floor
    )
    cos_one = displacement[0] / planar
    sin_one = displacement[1] / planar

    def neighbour_sum(values):
        weighted = values * radial[:, None, None]
        return jnp.sum(
            weighted.reshape(atom_count, neighbour_count, values.shape[1], feature_width), axis=1
        )

    collected = {}
    zero_slots = [layout.index(harmonic_slot(degree, 0)) for degree in range(5)]
    zero_input = source[:, zero_slots, :].reshape(edge_count, 5 * feature_width)
    zero_output = jnp.dot(zero_input, order_zero, preferred_element_type=jnp.float32)
    summed_zero_part = neighbour_sum(zero_output.reshape(edge_count, 5, feature_width))
    for degree in range(5):
        collected[harmonic_slot(degree, 0)] = summed_zero_part[:, degree]
    rotations = (
        (1, cos_one, sin_one, order_one),
        (2, cos_one * cos_one - sin_one * sin_one, 2.0 * cos_one * sin_one, order_two),
    )
    for harmonic_order, cosine, sine_term, weight_pair in rotations:
        degrees = list(range(harmonic_order, 5))
        count_of_rows = len(degrees)
        plus_slots = [layout.index(harmonic_slot(degree, harmonic_order)) for degree in degrees]
        minus_slots = [layout.index(harmonic_slot(degree, -harmonic_order)) for degree in degrees]
        plus_part = source[:, plus_slots, :].astype(jnp.float32)
        minus_part = source[:, minus_slots, :].astype(jnp.float32)
        cosine_wide = cosine[:, None, None]
        sine_wide = sine_term[:, None, None]
        turned_plus = (cosine_wide * plus_part + sine_wide * minus_part).astype(jnp.bfloat16)
        turned_minus = (cosine_wide * minus_part - sine_wide * plus_part).astype(jnp.bfloat16)
        split_at = count_of_rows * feature_width
        stacked = jnp.concatenate(
            [turned_plus.reshape(edge_count, split_at), turned_minus.reshape(edge_count, split_at)],
            axis=0,
        )
        product = jnp.dot(stacked, weight_pair, preferred_element_type=jnp.float32)
        upper_half = product[:edge_count]
        lower_half = product[edge_count:]
        mixed_plus = (upper_half[:, :split_at] - lower_half[:, split_at:]).reshape(
            edge_count, count_of_rows, feature_width
        )
        mixed_minus = (upper_half[:, split_at:] + lower_half[:, :split_at]).reshape(
            edge_count, count_of_rows, feature_width
        )
        back_plus = neighbour_sum(cosine_wide * mixed_plus - sine_wide * mixed_minus)
        back_minus = neighbour_sum(sine_wide * mixed_plus + cosine_wide * mixed_minus)
        for position_in, degree in enumerate(degrees):
            collected[harmonic_slot(degree, harmonic_order)] = back_plus[:, position_in]
            collected[harmonic_slot(degree, -harmonic_order)] = back_minus[:, position_in]
    zero_block = jnp.zeros((atom_count, feature_width), jnp.float32)
    return jnp.stack([collected.get(slot_number, zero_block) for slot_number in range(25)], axis=1)


def table_product(table, values):
    return jnp.dot(table.T, values, precision=highest)


def local(
    node_irreps,
    positions,
    send_list,
    neighbours,
    displacements,
    order_zero,
    order_one,
    order_two,
    reciprocal_triples,
    reciprocal_filter,
    cotangent,
):
    local_irreps = node_irreps[0, 0, 0]
    atom_count = local_irreps.shape[0]
    size_x = lax.axis_size("gx")
    size_y = lax.axis_size("gy")
    size_z = lax.axis_size("gz")
    total_atom_count = atom_count * size_x * size_y * size_z
    scale_factor = 1.0 / math.sqrt(total_atom_count * reciprocal_filter.shape[0])
    corner = jnp.stack([lax.axis_index("gx"), lax.axis_index("gy"), lax.axis_index("gz")]).astype(
        jnp.float32
    )
    box = cell_length * jnp.array([size_x, size_y, size_z], jnp.float32)
    fractional = (positions[0, 0, 0] + cell_length * corner[:, None]) / box[:, None]
    wave_float = reciprocal_triples.astype(jnp.float32)
    phase = 2.0 * math.pi * jnp.dot(fractional.T, wave_float.T, precision=highest)
    cos_table = jnp.cos(phase)
    sin_table = jnp.sin(phase)
    charges = local_irreps[:, 0, :].astype(jnp.float32)
    grad_input = cotangent[0, 0, 0]
    raw_cos, raw_sin, charge_total, plane_cos, plane_sin = lax.psum(
        (
            table_product(cos_table, charges),
            table_product(sin_table, charges),
            jnp.sum(charges, axis=0),
            jnp.sum(cos_table, axis=0),
            jnp.sum(sin_table, axis=0),
        ),
        ("gx", "gy", "gz"),
    )
    resp_cos, resp_sin = lax.psum(
        (table_product(cos_table, grad_input), table_product(sin_table, grad_input)),
        ("gx", "gy", "gz"),
    )
    mean_charge = charge_total / total_atom_count
    centered = charges - mean_charge
    struct_cos = raw_cos - plane_cos[:, None] * mean_charge[None, :]
    struct_sin = raw_sin - plane_sin[:, None] * mean_charge[None, :]
    sent_rows = send_list[0, 0, 0]
    layout = kept_rows()
    arrived = with_halo(
        local_irreps[sent_rows][None, None, None], (("gx", 0), ("gy", 1), ("gz", 2)), 1
    )
    ghost_table = arrived.reshape((-1,) + local_irreps.shape[1:])
    lookup_table = jnp.concatenate([local_irreps, ghost_table], axis=0)
    messages = edge_messages(
        lookup_table,
        displacements[0, 0, 0],
        neighbours[0, 0, 0],
        order_zero,
        order_one,
        order_two,
        layout,
    )
    updated = (local_irreps.astype(jnp.float32) + messages).astype(jnp.bfloat16)
    long_range = scale_factor * (
        jnp.dot(cos_table, reciprocal_filter * struct_cos, precision=highest)
        + jnp.dot(sin_table, reciprocal_filter * struct_sin, precision=highest)
    )
    charge_term = scale_factor * (
        jnp.dot(cos_table, reciprocal_filter * resp_cos, precision=highest)
        + jnp.dot(sin_table, reciprocal_filter * resp_sin, precision=highest)
    )
    term_mean = (
        scale_factor
        * (
            jnp.dot(plane_cos, reciprocal_filter * resp_cos, precision=highest)
            + jnp.dot(plane_sin, reciprocal_filter * resp_sin, precision=highest)
        )
        / total_atom_count
    )
    charge_grad = charge_term - term_mean
    with_sin = jnp.dot(grad_input, (reciprocal_filter * struct_sin).T, precision=highest) + jnp.dot(
        centered, (reciprocal_filter * resp_sin).T, precision=highest
    )
    with_cos = jnp.dot(grad_input, (reciprocal_filter * struct_cos).T, precision=highest) + jnp.dot(
        centered, (reciprocal_filter * resp_cos).T, precision=highest
    )
    phase_grad = scale_factor * (cos_table * with_sin - sin_table * with_cos)
    position_grad = (2.0 * math.pi * jnp.dot(phase_grad, wave_float, precision=highest) / box).T
    return (
        updated[None, None, None],
        long_range[None, None, None],
        charge_grad[None, None, None],
        position_grad[None, None, None],
    )


def solution(mesh):
    return jax.shard_map(
        local,
        mesh=mesh,
        in_specs=(
            P("gx", "gy", "gz", None, None, None),
            P("gx", "gy", "gz", None, None),
            P("gx", "gy", "gz", None),
            P("gx", "gy", "gz", None, None),
            P("gx", "gy", "gz", None, None),
            P(),
            P(),
            P(),
            P(),
            P(),
            P("gx", "gy", "gz", None, None),
        ),
        out_specs=(
            P("gx", "gy", "gz", None, None, None),
            P("gx", "gy", "gz", None, None),
            P("gx", "gy", "gz", None, None),
            P("gx", "gy", "gz", None, None),
        ),
        check_vma=False,
    )
```

profile of v0, /device:TPU:0, one launch (start us, length us, event | category | flops | bytes accessed | tf_op | source)
XLA Modules:
  0.0 176.4 jit_solution(5121559690905927124)
XLA Ops:
  7.2 0.7 fusion.51
  8.0 0.9 copy.82
  9.5 5.1 %collective-permute-start.1 = (bf16[1,1,1,8,25,128]{5,4,3,2,1,0:T(8,128)(2,1)S(1)}, bf16[1,1,1,8,25,128]{5,4,3,2,1,0:T(8,128)(2,1)S(1)}, u32[]{:S(2)}, u32[]{:S(2)}) collective-permute-start(bf16[1,1,1,8,25,128]{5,4,3,2,1,0:T(8,128)(2,1)S(1)} %bitcast.173), channel_id=1, source_target_pairs={{8,0},{16,8},{24,16},{0,24},{9,1},{17,9},{25,17},{1,25},{10,2},{18... | collective-permute-start | bytes 153608 | tf_op jit(solution)/shard_map/ppermute | solution.py:22
  14.7 1.3 fusion.62
  16.1 1.4 fusion.40
  17.5 1.4 fusion.42
  18.9 2.5 %fusion.34 = f32[1024,128]{1,0:T(8,128)} fusion(f32[16,1024]{1,0:T(8,128)S(1)} %get-tuple-element.43, f32[1,1,1,16,128]{4,3,2,1,0:T(8,128)} %param.27), kind=kOutput, calls=%fused_computation.112 | convolution fusion | flops 25165824 | bytes 598016 | tf_op jit(solution)/shard_map/dot_general | solution.py:108
  21.4 1.8 %fusion.36 = f32[1024,128]{1,0:T(8,128)} fusion(f32[16,1024]{1,0:T(8,128)S(1)} %get-tuple-element.44, f32[1,1,1,16,128]{4,3,2,1,0:T(8,128)S(1)} %copy-done.11), kind=kOutput, calls=%fused_computation.114 | convolution fusion | flops 25165824 | bytes 598016 | tf_op jit(solution)/shard_map/dot_general | solution.py:108
  23.5 40.4 %all-reduce = (f32[128]{0:T(128)S(1)}, f32[1024]{0:T(1024)S(1)}, f32[1024]{0:T(1024)S(1)}) all-reduce(f32[128]{0:T(128)S(1)} %get-tuple-element.33, f32[1024]{0:T(1024)S(1)} %reduce_sum.87, f32[1024]{0:T(1024)S(1)} %reduce_sum.89), channel_id=1, replica_groups=mesh['gx'=4,'gy'=4,'gz'=2] {'gx','gy','gz'}, use_global_device_ids=true, to_apply=%region_10.0 | all-reduce | flops 2176 | bytes 17408 | tf_op jit(solution)/shard_map/psum | solution.py:142
  64.5 3.0 %collective-permute-done.3 = bf16[3,1,1,8,25,128]{5,4,3,2,1,0:T(8,128)(2,1)S(1)} collective-permute-done((bf16[3,1,1,8,25,128]{5,4,3,2,1,0:T(8,128)(2,1)S(1)}, bf16[3,1,1,8,25,128]{5,4,3,2,1,0:T(8,128)(2,1)S(1)}, u32[]{:S(2)}, u32[]{:S(2)}) %collective-permute-start.3) | collective-permute-done | bytes 153632 | tf_op jit(solution)/shard_map/ppermute | solution.py:22
  67.5 4.2 %collective-permute-done.2 = bf16[3,1,1,8,25,128]{5,4,3,2,1,0:T(8,128)(2,1)S(1)} collective-permute-done((bf16[3,1,1,8,25,128]{5,4,3,2,1,0:T(8,128)(2,1)S(1)}, bf16[3,1,1,8,25,128]{5,4,3,2,1,0:T(8,128)(2,1)S(1)}, u32[]{:S(2)}, u32[]{:S(2)}) %collective-permute-start.2) | collective-permute-done | bytes 153632 | tf_op jit(solution)/shard_map/ppermute | solution.py:19
  72.0 1.0 collective-permute-start.5
  73.0 1.1 collective-permute-start.4
  74.3 1.5 copy.58
  77.1 8.9 %collective-permute-done.5 = bf16[3,3,1,8,25,128]{5,3,4,2,1,0:T(8,128)(2,1)} collective-permute-done((bf16[3,3,1,8,25,128]{5,3,4,2,1,0:T(8,128)(2,1)S(1)}, bf16[3,3,1,8,25,128]{5,3,4,2,1,0:T(8,128)(2,1)}, u32[]{:S(2)}, u32[]{:S(2)}) %collective-permute-start.5) | collective-permute-done | bytes 460832 | tf_op jit(solution)/shard_map/ppermute | solution.py:22
  85.9 1.1 copy.53
  87.1 8.1 %collective-permute-done.4 = bf16[3,3,1,8,25,128]{5,3,4,2,1,0:T(8,128)(2,1)} collective-permute-done((bf16[3,3,1,8,25,128]{5,3,4,2,1,0:T(8,128)(2,1)S(1)}, bf16[3,3,1,8,25,128]{5,3,4,2,1,0:T(8,128)(2,1)}, u32[]{:S(2)}, u32[]{:S(2)}) %collective-permute-start.4) | collective-permute-done | bytes 460832 | tf_op jit(solution)/shard_map/ppermute | solution.py:19
  95.2 1.1 copy.52
  96.9 3.5 %gather_fusion.1 = bf16[512,25,128]{2,1,0:T(8,128)(2,1)} fusion(bf16[232,25,128]{2,1,0:T(8,128)(2,1)S(1)} %pad_maximum_fusion, s32[1024]{0:T(1024)S(1)} %get-tuple-element.75), kind=kCustom, calls=%fused_computation.1 | custom fusion | bytes 6555648 | tf_op jit(solution)/shard_map/gather | solution.py:47
  100.3 5.2 %copy.56 = bf16[512,25,128]{2,0,1:T(8,128)(2,1)} copy(bf16[512,25,128]{2,1,0:T(8,128)(2,1)} %gather_fusion.1) | data formatting | bytes 6553600 | tf_op jit(solution)/shard_map/gather | solution.py:47
  105.5 3.3 %gather_fusion.6 = bf16[3,512,128]{2,1,0:T(8,128)(2,1)} fusion(bf16[512,25,128]{2,0,1:T(8,128)(2,1)} %copy.56, s32[1024]{0:T(1024)S(1)} %get-tuple-element.70), kind=kCustom, calls=%fused_computation.6 | custom fusion | bytes 786444 | tf_op jit(solution)/shard_map/gather | solution.py:79
  108.8 2.5 %gather_fusion.5 = bf16[3,512,128]{2,1,0:T(8,128)(2,1)S(1)} fusion(bf16[512,25,128]{2,0,1:T(8,128)(2,1)} %copy.56, s32[1024]{0:T(1024)S(1)} %get-tuple-element.71), kind=kCustom, calls=%fused_computation.5 | custom fusion | bytes 786444 | tf_op jit(solution)/shard_map/gather | solution.py:78
  111.7 1.0 convert_bitcast_fusion.2
  112.7 1.2 copy.67
  113.9 3.4 %gather_fusion.4 = bf16[4,512,128]{2,1,0:T(8,128)(2,1)} fusion(bf16[512,25,128]{2,0,1:T(8,128)(2,1)} %copy.56, s32[1024]{0:T(1024)S(1)} %get-tuple-element.72), kind=kCustom, calls=%fused_computation.4 | custom fusion | bytes 1048592 | tf_op jit(solution)/shard_map/gather | solution.py:79
  117.3 3.4 %gather_fusion.3 = bf16[4,512,128]{2,1,0:T(8,128)(2,1)} fusion(bf16[512,25,128]{2,0,1:T(8,128)(2,1)} %copy.56, s32[1024]{0:T(1024)S(1)} %get-tuple-element.73), kind=kCustom, calls=%fused_computation.3 | custom fusion | bytes 1048592 | tf_op jit(solution)/shard_map/gather | solution.py:78
  120.7 2.6 %gather_fusion.2 = bf16[5,512,128]{2,1,0:T(8,128)(2,1)S(1)} fusion(bf16[512,25,128]{2,0,1:T(8,128)(2,1)} %copy.56, s32[1024]{0:T(1024)S(1)} %get-tuple-element.74), kind=kCustom, calls=%fused_computation.2 | custom fusion | bytes 1310740 | tf_op jit(solution)/shard_map/gather | solution.py:64
  123.3 1.1 copy.57
  124.4 2.2 %bitcast_reduce_fusion = f32[16,5,128]{2,0,1:T(8,128)S(1)} fusion(f32[512]{0:T(512)S(1)} %exponential_multiply_fusion, bf16[512,640,1]{0,1,2:T(8,128)(2,1)} %bitcast.182, bf16[5,128,640]{2,1,0:T(8,128)(2,1)} %bitcast.181), kind=kOutput, calls=%fused_computation.10 | convolution fusion | flops 420075520 | bytes 1517568 | tf_op jit(solution)/shard_map/dot_general | solution.py:65
  126.7 1.3 copy.61
  128.0 1.1 convert_bitcast_fusion
  129.1 1.3 copy.63
  130.5 1.4 fusion.26
  131.9 1.0 fusion.21
  132.9 1.0 slice_subtract_fusion.1
  134.3 1.5 reshape.294
  135.8 3.1 %multiply_reduce_fusion = (f32[16,3,128]{2,1,0:T(4,128)S(1)}, f32[16,3,128]{2,1,0:T(4,128)S(1)}) fusion(f32[16,32,3,128]{3,2,1,0:T(4,128)S(1)} %reshape.294, f32[16,32,3,128]{3,2,1,0:T(4,128)S(1)} %reshape.293, f32[16,32]{1,0:T(8,128)S(1)} %div.88, f32[16,32]{1,0:T(8,128)} %get-tuple-element.60, f32[16,32]{1,0:T(8,128)} %get-tuple-element.59), kind=kLoop, calls=%fused_computation.50 | loop fusion | flops 1953792 | bytes 1628160 | tf_op jit(solution)/shard_map/reduce_sum | solution.py:58
  139.3 1.3 fusion.13
  140.6 1.8 %slice_subtract_fusion = (f32[512,512]{1,0:T(8,128)}, f32[512,512]{1,0:T(8,128)}) fusion(f32[1024,1024]{1,0:T(8,128)S(1)} %fusion.13), kind=kLoop, calls=%fused_computation.35 | loop fusion | flops 524288 | bytes 6291456 | tf_op jit(solution)/shard_map/sub | solution.py:92
  142.4 1.6 reshape.291
  144.1 2.6 %reshape.292 = f32[16,32,4,128]{3,2,1,0:T(4,128)} reshape(f32[512,512]{1,0:T(8,128)} %get-tuple-element.36) | data formatting | bytes 2097152 | tf_op jit(solution)/shard_map/reshape | solution.py:95
  146.7 3.7 %multiply_reduce_fusion.2 = (f32[16,4,128]{2,1,0:T(4,128)S(1)}, f32[16,4,128]{2,1,0:T(4,128)S(1)}) fusion(f32[16,32,4,128]{3,2,1,0:T(4,128)} %reshape.292, f32[16,32,4,128]{3,2,1,0:T(4,128)S(1)} %reshape.291, f32[16,32]{1,0:T(8,128)S(1)} %div.88, f32[16,32]{1,0:T(8,128)S(1)} %copy-done.13, f32[16,32]{1,0:T(8,128)S(1)} %copy-done.14), kind=kLoop, calls=%fused_computation.52 | loop fusion | flops 2605056 | bytes 2168832 | tf_op jit(solution)/shard_map/reduce_sum | solution.py:58
  151.3 8.9 %all-reduce.4.cloned.1.call-done = (f32[1024,128]{1,0:T(8,128)}, f32[1024,128]{1,0:T(8,128)}, f32[1024,128]{1,0:T(8,128)}, f32[1024,128]{1,0:T(8,128)}) async-done(((f32[1024,128]{1,0:T(8,128)}, f32[1024,128]{1,0:T(8,128)}, f32[1024,128]{1,0:T(8,128)}, f32[1024,128]{1,0:T(8,128)}), (f32[1024,128]{1,0:T(8,128)}, f32[1024,128]{1,0:T(8,128)}, f32[1024,128]{1,0:T(8,128)}, ...) | async-done | bytes 2097168 | tf_op jit(solution)/shard_map/psum | solution.py:142
  160.3 1.6 fusion.29
  161.8 1.7 convolution_bitcast_fusion
  165.0 0.7 convolution_bitcast_fusion.1
  165.7 1.1 fusion.8
  168.5 1.0 fusion.6
  (127 shorter events, 8.8 us)
Async XLA Ops:
  7.2 132.1 %copy-start = (bf16[512,1024]{1,0:T(8,128)(2,1)S(1)}, bf16[512,1024]{1,0:T(8,128)(2,1)}, u32[]{:S(2)}) copy-start(bf16[512,1024]{1,0:T(8,128)(2,1)} %param.23) | copy-start | bytes 3145732
  7.2 14.2 %copy-start.11 = (f32[1,1,1,16,128]{4,3,2,1,0:T(8,128)S(1)}, f32[1,1,1,16,128]{4,3,2,1,0:T(8,128)}, u32[]{:S(2)}) copy-start(f32[1,1,1,16,128]{4,3,2,1,0:T(8,128)} %param.27) | copy-start | bytes 24580
  7.2 153.1 %all-reduce.4.cloned.1.call-start = ((), (), s32[]{:S(2)}) async-start(), calls=%async_computation | async-start | bytes 4194304 | tf_op jit(solution)/shard_map/psum | solution.py:142
  9.5 54.4 %collective-permute-start.1 = (bf16[1,1,1,8,25,128]{5,4,3,2,1,0:T(8,128)(2,1)S(1)}, bf16[1,1,1,8,25,128]{5,4,3,2,1,0:T(8,128)(2,1)S(1)}, u32[]{:S(2)}, u32[]{:S(2)}) collective-permute-start(bf16[1,1,1,8,25,128]{5,4,3,2,1,0:T(8,128)(2,1)S(1)} %bitcast.173), channel_id=1, source_target_pairs={{8,0},{16,8},{24,16},{0,24},{9,1},{17,9},{25,17},{1,25},{10,2},{18... | collective-permute-start | bytes 153608 | tf_op jit(solution)/shard_map/ppermute | solution.py:22
  14.6 49.3 %collective-permute-start = (bf16[1,1,1,8,25,128]{5,4,3,2,1,0:T(8,128)(2,1)S(1)}, bf16[1,1,1,8,25,128]{5,4,3,2,1,0:T(8,128)(2,1)S(1)}, u32[]{:S(2)}, u32[]{:S(2)}) collective-permute-start(bf16[1,1,1,8,25,128]{5,4,3,2,1,0:T(8,128)(2,1)S(1)} %bitcast.174), channel_id=1, source_target_pairs={{0,8},{8,16},{16,24},{24,0},{1,9},{9,17},{17,25},{25,1},{2,10},{10... | collective-permute-start | bytes 153608 | tf_op jit(solution)/shard_map/ppermute | solution.py:19
  17.5 5.8 %copy-start.15 = (f32[1,1,1,3,512]{4,2,3,1,0:T(1,128)S(1)}, f32[1,1,1,3,512]{4,2,3,1,0:T(1,128)}, u32[]{:S(2)}) copy-start(f32[1,1,1,3,512]{4,2,3,1,0:T(1,128)} %param.21) | copy-start | bytes 18436
  17.5 5.9 %copy-start.20 = (s32[1,1,1,16,32]{4,3,2,1,0:T(8,128)S(1)}, s32[1,1,1,16,32]{4,3,2,1,0:T(8,128)}, u32[]{:S(2)}) copy-start(s32[1,1,1,16,32]{4,3,2,1,0:T(8,128)} %param.20) | copy-start | bytes 6148
  18.9 45.6 %copy-start.26 = (s32[5]{0:T(128)S(1)}, s32[5]{0:T(128)}, u32[]{:S(2)}) copy-start(s32[5]{0:T(128)} %constant.102) | copy-start | bytes 64
  18.9 45.6 %copy-start.24 = (s32[4]{0:T(128)S(1)}, s32[4]{0:T(128)}, u32[]{:S(2)}) copy-start(s32[4]{0:T(128)} %constant.104) | copy-start | bytes 52
  18.9 45.7 %copy-start.25 = (s32[4]{0:T(128)S(1)}, s32[4]{0:T(128)}, u32[]{:S(2)}) copy-start(s32[4]{0:T(128)} %constant.103) | copy-start | bytes 52
  23.2 50.8 %copy-start.22 = (s32[3]{0:T(128)S(1)}, s32[3]{0:T(128)}, u32[]{:S(2)}) copy-start(s32[3]{0:T(128)} %constant.106) | copy-start | bytes 40
  23.3 50.8 %copy-start.23 = (s32[3]{0:T(128)S(1)}, s32[3]{0:T(128)}, u32[]{:S(2)}) copy-start(s32[3]{0:T(128)} %constant.105) | copy-start | bytes 40
  23.3 51.1 %copy-start.8 = (bf16[640,640]{1,0:T(8,128)(2,1)S(1)}, bf16[640,640]{1,0:T(8,128)(2,1)}, u32[]{:S(2)}) copy-start(bf16[640,640]{1,0:T(8,128)(2,1)} %param.22) | copy-start | bytes 2457604
  63.9 3.6 %collective-permute-start.3 = (bf16[3,1,1,8,25,128]{5,4,3,2,1,0:T(8,128)(2,1)S(1)}, bf16[3,1,1,8,25,128]{5,4,3,2,1,0:T(8,128)(2,1)S(1)}, u32[]{:S(2)}, u32[]{:S(2)}) collective-permute-start(bf16[3,1,1,8,25,128]{5,4,3,2,1,0:T(8,128)(2,1)S(1)} %pad_maximum_fusion.3), channel_id=1, source_target_pairs={{2,0},{4,2},{6,4},{0,6},{3,1},{5,3},{7,5},{1,7},{10,8},{12,10},{14... | collective-permute-start | bytes 460808 | tf_op jit(solution)/shard_map/ppermute | solution.py:22
  64.0 7.7 %collective-permute-start.2 = (bf16[3,1,1,8,25,128]{5,4,3,2,1,0:T(8,128)(2,1)S(1)}, bf16[3,1,1,8,25,128]{5,4,3,2,1,0:T(8,128)(2,1)S(1)}, u32[]{:S(2)}, u32[]{:S(2)}) collective-permute-start(bf16[3,1,1,8,25,128]{5,4,3,2,1,0:T(8,128)(2,1)S(1)} %pad_maximum_fusion.3), channel_id=1, source_target_pairs={{0,2},{2,4},{4,6},{6,0},{1,3},{3,5},{5,7},{7,1},{8,10},{10,12},{12... | collective-permute-start | bytes 460808 | tf_op jit(solution)/shard_map/ppermute | solution.py:19
  72.0 14.0 %collective-permute-start.5 = (bf16[3,3,1,8,25,128]{5,3,4,2,1,0:T(8,128)(2,1)S(1)}, bf16[3,3,1,8,25,128]{5,3,4,2,1,0:T(8,128)(2,1)}, u32[]{:S(2)}, u32[]{:S(2)}) collective-permute-start(bf16[3,3,1,8,25,128]{5,3,4,2,1,0:T(8,128)(2,1)S(1)} %copy.50), channel_id=1, source_target_pairs={{1,0},{0,1},{3,2},{2,3},{5,4},{4,5},{7,6},{6,7},{9,8},{8,9},{11,10... | collective-permute-start | bytes 1382408 | tf_op jit(solution)/shard_map/ppermute | solution.py:22
  73.0 22.2 %collective-permute-start.4 = (bf16[3,3,1,8,25,128]{5,3,4,2,1,0:T(8,128)(2,1)S(1)}, bf16[3,3,1,8,25,128]{5,3,4,2,1,0:T(8,128)(2,1)}, u32[]{:S(2)}, u32[]{:S(2)}) collective-permute-start(bf16[3,3,1,8,25,128]{5,3,4,2,1,0:T(8,128)(2,1)S(1)} %copy.50), channel_id=1, source_target_pairs={{0,1},{1,0},{2,3},{3,2},{4,5},{5,4},{6,7},{7,6},{8,9},{9,8},{10,11... | collective-permute-start | bytes 1382408 | tf_op jit(solution)/shard_map/ppermute | solution.py:19
  124.4 2.2 %copy-start.6 = (bf16[4,512,128]{2,1,0:T(8,128)(2,1)S(1)}, bf16[4,512,128]{2,1,0:T(8,128)(2,1)}, u32[]{:S(2)}) copy-start(bf16[4,512,128]{2,1,0:T(8,128)(2,1)} %gather_fusion.3) | copy-start | bytes 1572868
  128.0 2.5 %copy-start.18 = (f32[512]{0:T(512)S(1)}, f32[512]{0:T(512)}, u32[]{:S(2)}) copy-start(f32[512]{0:T(512)} %get-tuple-element.65) | copy-start | bytes 6148
  128.0 2.5 %copy-start.19 = (f32[512]{0:T(512)S(1)}, f32[512]{0:T(512)}, u32[]{:S(2)}) copy-start(f32[512]{0:T(512)} %get-tuple-element.68) | copy-start | bytes 6148
  130.5 1.4 copy-start.9
  135.7 3.2 %copy-start.4 = (f32[512,4,128]{0,2,1:T(8,128)S(1)}, f32[512,4,128]{0,2,1:T(8,128)}, u32[]{:S(2)}) copy-start(f32[512,4,128]{0,2,1:T(8,128)} %copy.61) | copy-start | bytes 3145732
  135.7 3.2 %copy-start.5 = (f32[512,4,128]{0,2,1:T(8,128)S(1)}, f32[512,4,128]{0,2,1:T(8,128)}, u32[]{:S(2)}) copy-start(f32[512,4,128]{0,2,1:T(8,128)} %copy.63) | copy-start | bytes 3145732
  135.8 3.2 %copy-start.16 = (f32[512]{0:T(512)S(1)}, f32[512]{0:T(512)}, u32[]{:S(2)}) copy-start(f32[512]{0:T(512)} %get-tuple-element.66) | copy-start | bytes 6148
  135.8 3.2 %copy-start.17 = (f32[512]{0:T(512)S(1)}, f32[512]{0:T(512)}, u32[]{:S(2)}) copy-start(f32[512]{0:T(512)} %get-tuple-element.67) | copy-start | bytes 6148
  142.4 4.2 %copy-start.13 = (f32[16,32]{1,0:T(8,128)S(1)}, f32[16,32]{1,0:T(8,128)}, u32[]{:S(2)}) copy-start(f32[16,32]{1,0:T(8,128)} %get-tuple-element.61) | copy-start | bytes 6148
  142.4 4.2 %copy-start.14 = (f32[16,32]{1,0:T(8,128)S(1)}, f32[16,32]{1,0:T(8,128)}, u32[]{:S(2)}) copy-start(f32[16,32]{1,0:T(8,128)} %get-tuple-element.62) | copy-start | bytes 6148
  144.0 6.6 %copy-start.10 = (bf16[1,1,1,16,25,128]{5,3,4,2,1,0:T(8,128)(2,1)S(1)}, bf16[1,1,1,16,25,128]{5,3,4,2,1,0:T(8,128)(2,1)}, u32[]{:S(2)}) copy-start(bf16[1,1,1,16,25,128]{5,3,4,2,1,0:T(8,128)(2,1)} %param.17) | copy-start | bytes 307204
  146.6 13.6 %copy-start.1 = (f32[1024,128]{1,0:T(8,128)S(1)}, f32[1024,128]{1,0:T(8,128)}, u32[]{:S(2)}) copy-start(f32[1024,128]{1,0:T(8,128)} %param.26) | copy-start | bytes 1572868
  160.2 3.3 %copy-start.3 = (f32[1024,128]{1,0:T(8,128)S(1)}, f32[1024,128]{1,0:T(8,128)}, u32[]{:S(2)}) copy-start(f32[1024,128]{1,0:T(8,128)} %get-tuple-element.31) | copy-start | bytes 1572868
  163.6 1.4 copy-start.7
  164.4 2.4 %copy-start.2 = (f32[1024,128]{1,0:T(8,128)S(1)}, f32[1024,128]{1,0:T(8,128)}, u32[]{:S(2)}) copy-start(f32[1024,128]{1,0:T(8,128)} %get-tuple-element.32) | copy-start | bytes 1572868
  165.0 2.4 %copy-start.12 = (s32[1024,3]{0,1:T(4,128)S(1)}, s32[1024,3]{0,1:T(4,128)}, u32[]{:S(2)}) copy-start(s32[1024,3]{0,1:T(4,128)} %param.25) | copy-start | bytes 36868
  165.0 2.4 %copy-start.21 = (f32[3]{0:T(128)S(1)}, f32[3]{0:T(128)}, u32[]{:S(2)}) copy-start(f32[3]{0:T(128)} %constant.100) | copy-start | bytes 40
Sparse Core Ops, SparseCore 0:
  23.4 136.8 all-reduce.3
where the time goes:
time: 177 us; the launch traced here: 176 us
  local copies, waits for them, and re-layouts  41.7 us (24%)
  blocking collectives  40.4 us (23%)
  waiting for transfers between devices  33.1 us (19%)
  matrix products  21.6 us (12%)
  other arithmetic  17.1 us (10%)
  between operations  14.7 us (8%)
  starting transfers between devices  7.82 us (4%)
    psum x1, blocking collectives, local(): lax.psum((table_product(cos_table, charges), table_product(sin_table, cha...  40.4 us
    ppermute x3, waiting for transfers between devices, with_halo(): lax.ppermute(lax.slice_in_dim(block, block.shape[dim] - width, None, axis...  12.3 us
    ppermute x3, waiting for transfers between devices, with_halo(): lax.ppermute(lax.slice_in_dim(block, 0, width, axis=dim), axis, backward)  11.8 us
    psum x1, waiting for transfers between devices, local(): lax.psum((table_product(cos_table, charges), table_product(sin_table, cha...  8.93 us
    gather x2, local copies, waits for them, and re-layouts, edge_messages(): source = lookup_table[flat_index]  8.67 us
    dot_general x4, matrix products, table_product(): return jnp.dot(table.T, values, precision=highest)  7.14 us
    reduce_sum x2, other arithmetic, neighbour_sum(): jnp.sum(weighted.reshape(atom_count, neighbour_count, values.shape[1], fe...  6.74 us
    gather x2, local copies, waits for them, and re-layouts, edge_messages(): minus_part = source[:, minus_slots, :].astype(jnp.float32)  6.71 us
  transfers between devices with their start and end apart: 7, of which 5 were waited for; matrix products, arithmetic and copies ran while one was open for 39% of the time, Pallas kernels for 0%

commit v1 on v0

--- a/solution.py
+++ b/solution.py
@@ -1,3 +1,4 @@
+import functools
 import math
 import jax
 import jax.numpy as jnp
@@ -8,6 +9,15 @@
 cell_length = 6.8
 planar_floor = 0.25
 radial_width = 64.0
+
+
+def roads_fit(buf, named_axis, comm_axis):
+    for jj in (named_axis, comm_axis):
+        buf = lax.psum(buf, jj)
+    return buf
+
+
+keep_up_things_here = functools.partial(roads_fit, named_axis=("gy", "gz"), comm_axis="gx")
 
 
 def with_halo(block, sides, width):
@@ -139,15 +149,14 @@
     sin_table = jnp.sin(phase)
     charges = local_irreps[:, 0, :].astype(jnp.float32)
     grad_input = cotangent[0, 0, 0]
-    raw_cos, raw_sin, charge_total, plane_cos, plane_sin = lax.psum(
+    raw_cos, raw_sin, charge_total, plane_cos, plane_sin = keep_up_things_here(
         (
             table_product(cos_table, charges),
             table_product(sin_table, charges),
             jnp.sum(charges, axis=0),
             jnp.sum(cos_table, axis=0),
             jnp.sum(sin_table, axis=0),
-        ),
-        ("gx", "gy", "gz"),
+        )
     )
     resp_cos, resp_sin = lax.psum(
         (table_product(cos_table, grad_input), table_product(sin_table, grad_input)),

time: 177 us -> 288 us (1.63)
  waiting for transfers between devices: 33.1 us -> 148 us
  blocking collectives: 40.4 us -> 27.4 us
  other arithmetic: 17.1 us -> 21.7 us
    psum x1 -> x3, waiting for transfers between devices: 8.93 us -> 143 us  [the longest x1 88.2 us: local(): lax.psum((table_product(cos_table, grad_input), table_product(sin_table,...]
    psum x1 -> x2, blocking collectives: 40.4 us -> 27.4 us  [roads_fit(): buf = lax.psum(buf, jj)]
    ppermute x3, waiting for transfers between devices: 11.8 us -> 1.67 us  [with_halo(): lax.ppermute(lax.slice_in_dim(block, 0, width, axis=dim), axis, backward)]
    ppermute x3, waiting for transfers between devices: 12.3 us -> 3.24 us  [with_halo(): lax.ppermute(lax.slice_in_dim(block, block.shape[dim] - width, None, axis...]
  transfers between devices with their start and end apart: 7 -> 9, of which waited for: 5 -> 4; matrix products, arithmetic and copies ran while one was open for 39% -> 28% of each run, Pallas kernels for 0% -> 0%
where the time goes in v1:
time: 288 us; the launch traced here: 287 us
  waiting for transfers between devices  148 us (51%)
  local copies, waits for them, and re-layouts  42.9 us (15%)
  blocking collectives  27.4 us (10%)
  matrix products  24.4 us (8%)
  other arithmetic  21.7 us (8%)
  between operations  14.6 us (5%)
  starting transfers between devices  7.9 us (3%)
    psum x1, waiting for transfers between devices, local(): lax.psum((table_product(cos_table, grad_input), table_product(sin_table,...  88.2 us
    psum x2, waiting for transfers between devices, roads_fit(): buf = lax.psum(buf, jj)  54.6 us
    psum x2, blocking collectives, roads_fit(): buf = lax.psum(buf, jj)  27.4 us
    gather x2, local copies, waits for them, and re-layouts, edge_messages(): source = lookup_table[flat_index]  8.91 us
    dot_general x4, matrix products, table_product(): return jnp.dot(table.T, values, precision=highest)  7.83 us
    reduce_sum x2, other arithmetic, neighbour_sum(): jnp.sum(weighted.reshape(atom_count, neighbour_count, values.shape[1], fe...  7.16 us
    gather x2, local copies, waits for them, and re-layouts, edge_messages(): minus_part = source[:, minus_slots, :].astype(jnp.float32)  6.9 us
    gather x2, local copies, waits for them, and re-layouts, edge_messages(): plus_part = source[:, plus_slots, :].astype(jnp.float32)  6.15 us
  transfers between devices with their start and end apart: 9, of which 4 were waited for; matrix products, arithmetic and copies ran while one was open for 28% of the time, Pallas kernels for 0%

profile of v1, /device:TPU:0, one launch (start us, length us, event | category | flops | bytes accessed | tf_op | source)
XLA Modules:
  0.0 286.6 jit_solution(14387929427936474369)
XLA Ops:
  9.5 5.1 %collective-permute-start.1 = (bf16[1,1,1,8,25,128]{5,4,3,2,1,0:T(8,128)(2,1)S(1)}, bf16[1,1,1,8,25,128]{5,4,3,2,1,0:T(8,128)(2,1)S(1)}, u32[]{:S(2)}, u32[]{:S(2)}) collective-permute-start(bf16[1,1,1,8,25,128]{5,4,3,2,1,0:T(8,128)(2,1)S(1)} %bitcast.173), channel_id=1, source_target_pairs={{8,0},{16,8},{24,16},{0,24},{9,1},{17,9},{25,17},{1,25},{10,2},{18... | collective-permute-start | bytes 153608 | tf_op jit(solution)/shard_map/ppermute | solution.py:32
  14.7 1.3 fusion.62
  16.0 2.5 fusion.34
  18.5 2.5 fusion.36
  21.2 1.4 fusion.40
  22.6 1.4 fusion.42
  24.4 14.4 %all-reduce.1 = (f32[128]{0:T(128)S(1)}, f32[1024]{0:T(1024)S(1)}, f32[1024]{0:T(1024)S(1)}) all-reduce(f32[128]{0:T(128)S(1)} %get-tuple-element.38, f32[1024]{0:T(1024)S(1)} %reduce_sum.87, f32[1024]{0:T(1024)S(1)} %reduce_sum.89), channel_id=1, replica_groups=mesh['gx'=4,'gy'=4,'gz'=2] {'gy','gz'}, use_global_device_ids=true, to_apply=%region_12.0 | all-reduce | flops 2176 | bytes 17408 | tf_op jit(solution)/shard_map/psum | solution.py:16
  38.9 13.0 %all-reduce.3 = (f32[128]{0:T(128)S(1)}, f32[1024]{0:T(1024)S(1)}, f32[1024]{0:T(1024)S(1)}) all-reduce(f32[128]{0:T(128)S(1)} %get-tuple-element.28, f32[1024]{0:T(1024)S(1)} %get-tuple-element.29, f32[1024]{0:T(1024)S(1)} %get-tuple-element.30), channel_id=1, replica_groups=mesh['gx'=4,'gy'=4,'gz'=2] {'gx'}, use_global_device_ids=true, to_apply=%region_13.0 | all-reduce | flops 2176 | bytes 17408 | tf_op jit(solution)/shard_map/psum | solution.py:16
  55.6 1.3 copy.58
  57.5 1.7 collective-permute-done.3
  59.2 3.2 %collective-permute-done.2 = bf16[3,1,1,8,25,128]{5,4,3,2,1,0:T(8,128)(2,1)} collective-permute-done((bf16[3,1,1,8,25,128]{5,4,3,2,1,0:T(8,128)(2,1)S(1)}, bf16[3,1,1,8,25,128]{5,4,3,2,1,0:T(8,128)(2,1)}, u32[]{:S(2)}, u32[]{:S(2)}) %collective-permute-start.2) | collective-permute-done | bytes 153632 | tf_op jit(solution)/shard_map/ppermute | solution.py:29
  62.4 1.0 pad_maximum_fusion.2
  64.1 1.7 collective-permute-start.4
  65.7 88.2 %all-reduce.9.cloned.1.call-done = (f32[1024,128]{1,0:T(8,128)}, f32[1024,128]{1,0:T(8,128)}) async-done(((f32[1024,128]{1,0:T(8,128)}, f32[1024,128]{1,0:T(8,128)}), (f32[1024,128]{1,0:T(8,128)}, f32[1024,128]{1,0:T(8,128)})) %all-reduce.9.cloned.1.call-update) | async-done | bytes 1048592 | tf_op jit(solution)/shard_map/psum | solution.py:161
  153.9 1.5 convolution_bitcast_fusion.3
  155.4 1.4 fusion.12
  157.3 1.0 fusion.6
  158.3 54.6 %all-reduce.11.cloned.1.call-done = (f32[1024,128]{1,0:T(8,128)}, f32[1024,128]{1,0:T(8,128)}) async-done(((f32[1024,128]{1,0:T(8,128)}, f32[1024,128]{1,0:T(8,128)}), (f32[1024,128]{1,0:T(8,128)}, f32[1024,128]{1,0:T(8,128)})) %all-reduce.11.cloned.1.call-update) | async-done | bytes 1048592 | tf_op jit(solution)/shard_map/psum | solution.py:16
  213.0 1.1 copy.53
  214.2 1.2 pad_maximum_fusion.1
  215.7 3.6 %gather_fusion.1 = bf16[512,25,128]{2,1,0:T(8,128)(2,1)} fusion(bf16[232,25,128]{2,1,0:T(8,128)(2,1)S(1)} %pad_maximum_fusion, s32[1024]{0:T(1024)} %get-tuple-element.80), kind=kCustom, calls=%fused_computation.1 | custom fusion | bytes 6555648 | tf_op jit(solution)/shard_map/gather | solution.py:57
  219.3 5.3 %copy.56 = bf16[512,25,128]{2,0,1:T(8,128)(2,1)} copy(bf16[512,25,128]{2,1,0:T(8,128)(2,1)} %gather_fusion.1) | data formatting | bytes 6553600 | tf_op jit(solution)/shard_map/gather | solution.py:57
  224.6 3.4 %gather_fusion.6 = bf16[3,512,128]{2,1,0:T(8,128)(2,1)} fusion(bf16[512,25,128]{2,0,1:T(8,128)(2,1)} %copy.56, s32[1024]{0:T(1024)} %get-tuple-element.75), kind=kCustom, calls=%fused_computation.6 | custom fusion | bytes 786444 | tf_op jit(solution)/shard_map/gather | solution.py:89
  228.0 2.7 gather_fusion.5
  231.1 1.1 convert_bitcast_fusion.2
  232.1 1.1 copy.67
  233.3 3.5 %gather_fusion.4 = bf16[4,512,128]{2,1,0:T(8,128)(2,1)} fusion(bf16[512,25,128]{2,0,1:T(8,128)(2,1)} %copy.56, s32[1024]{0:T(1024)} %get-tuple-element.77), kind=kCustom, calls=%fused_computation.4 | custom fusion | bytes 1048592 | tf_op jit(solution)/shard_map/gather | solution.py:89
  236.8 3.5 %gather_fusion.3 = bf16[4,512,128]{2,1,0:T(8,128)(2,1)} fusion(bf16[512,25,128]{2,0,1:T(8,128)(2,1)} %copy.56, s32[1024]{0:T(1024)} %get-tuple-element.78), kind=kCustom, calls=%fused_computation.3 | custom fusion | bytes 1048592 | tf_op jit(solution)/shard_map/gather | solution.py:88
  240.2 2.7 gather_fusion.2
  242.9 1.1 copy.57
  244.0 2.2 bitcast_reduce_fusion
  246.9 1.3 copy.61
  248.3 1.1 convert_bitcast_fusion
  249.4 1.3 copy.63
  250.7 1.4 fusion.26
  252.1 1.0 fusion.21
  253.1 1.0 slice_subtract_fusion.1
  254.2 1.5 reshape.293
  255.7 1.3 reshape.294
  257.0 3.8 %multiply_reduce_fusion = (f32[16,3,128]{2,1,0:T(4,128)S(1)}, f32[16,3,128]{2,1,0:T(4,128)S(1)}) fusion(f32[16,32,3,128]{3,2,1,0:T(4,128)} %reshape.294, f32[16,32,3,128]{3,2,1,0:T(4,128)S(1)} %reshape.293, f32[16,32]{1,0:T(8,128)S(1)} %div.88, f32[16,32]{1,0:T(8,128)S(1)} %copy-done.25, f32[16,32]{1,0:T(8,128)S(1)} %copy-done.24), kind=kLoop, calls=%fused_computation.50 | loop fusion | flops 1953792 | bytes 1628160 | tf_op jit(solution)/shard_map/reduce_sum | solution.py:68
  261.2 1.3 fusion.13
  262.5 1.8 slice_subtract_fusion
  264.3 1.6 reshape.291
  265.9 2.6 reshape.292
  268.6 3.4 %multiply_reduce_fusion.2 = (f32[16,4,128]{2,1,0:T(4,128)S(1)}, f32[16,4,128]{2,1,0:T(4,128)S(1)}) fusion(f32[16,32,4,128]{3,2,1,0:T(4,128)} %reshape.292, f32[16,32,4,128]{3,2,1,0:T(4,128)S(1)} %reshape.291, f32[16,32]{1,0:T(8,128)S(1)} %div.88, f32[16,32]{1,0:T(8,128)S(1)} %copy-done.22, f32[16,32]{1,0:T(8,128)S(1)} %copy-done.23), kind=kLoop, calls=%fused_computation.52 | loop fusion | flops 2605056 | bytes 2168832 | tf_op jit(solution)/shard_map/reduce_sum | solution.py:68
  273.0 1.6 fusion.29
  274.6 1.8 convolution_bitcast_fusion
  277.1 1.1 fusion.8
  (162 shorter events, 13.3 us)
Async XLA Ops:
  7.2 254.0 %copy-start = (bf16[512,1024]{1,0:T(8,128)(2,1)S(1)}, bf16[512,1024]{1,0:T(8,128)(2,1)}, u32[]{:S(2)}) copy-start(bf16[512,1024]{1,0:T(8,128)(2,1)} %param.23) | copy-start | bytes 3145732
  7.2 146.7 %all-reduce.9.cloned.1.call-start = ((), (), s32[]{:S(2)}) async-start(), calls=%async_computation | async-start | bytes 2097152 | tf_op jit(solution)/shard_map/psum | solution.py:161
  8.9 15.1 %copy-start.12 = (bf16[1,1,1,16,25,128]{5,4,3,2,1,0:T(8,128)(2,1)}, bf16[1,1,1,16,25,128]{5,4,3,2,1,0:T(8,128)(2,1)S(1)}, u32[]{:S(2)}) copy-start(bf16[1,1,1,16,25,128]{5,4,3,2,1,0:T(8,128)(2,1)S(1)} %copy.82) | copy-start | bytes 307204
  9.5 44.8 %collective-permute-start.1 = (bf16[1,1,1,8,25,128]{5,4,3,2,1,0:T(8,128)(2,1)S(1)}, bf16[1,1,1,8,25,128]{5,4,3,2,1,0:T(8,128)(2,1)S(1)}, u32[]{:S(2)}, u32[]{:S(2)}) collective-permute-start(bf16[1,1,1,8,25,128]{5,4,3,2,1,0:T(8,128)(2,1)S(1)} %bitcast.173), channel_id=1, source_target_pairs={{8,0},{16,8},{24,16},{0,24},{9,1},{17,9},{25,17},{1,25},{10,2},{18... | collective-permute-start | bytes 153608 | tf_op jit(solution)/shard_map/ppermute | solution.py:32
  14.6 39.7 %collective-permute-start = (bf16[1,1,1,8,25,128]{5,4,3,2,1,0:T(8,128)(2,1)S(1)}, bf16[1,1,1,8,25,128]{5,4,3,2,1,0:T(8,128)(2,1)S(1)}, u32[]{:S(2)}, u32[]{:S(2)}) collective-permute-start(bf16[1,1,1,8,25,128]{5,4,3,2,1,0:T(8,128)(2,1)S(1)} %bitcast.174), channel_id=1, source_target_pairs={{0,8},{8,16},{16,24},{24,0},{1,9},{9,17},{17,25},{25,1},{2,10},{10... | collective-permute-start | bytes 153608 | tf_op jit(solution)/shard_map/ppermute | solution.py:29
  16.0 141.3 %copy-start.8 = (f32[16,1024]{1,0:T(8,128)}, f32[16,1024]{1,0:T(8,128)S(1)}, u32[]{:S(2)}) copy-start(f32[16,1024]{1,0:T(8,128)S(1)} %get-tuple-element.48) | copy-start | bytes 196612
  18.5 5.5 %copy-start.27 = (f32[1,1,1,3,512]{4,2,3,1,0:T(1,128)S(1)}, f32[1,1,1,3,512]{4,2,3,1,0:T(1,128)}, u32[]{:S(2)}) copy-start(f32[1,1,1,3,512]{4,2,3,1,0:T(1,128)} %param.21) | copy-start | bytes 18436
  18.5 5.6 %copy-start.32 = (s32[1,1,1,16,32]{4,3,2,1,0:T(8,128)S(1)}, s32[1,1,1,16,32]{4,3,2,1,0:T(8,128)}, u32[]{:S(2)}) copy-start(s32[1,1,1,16,32]{4,3,2,1,0:T(8,128)} %param.20) | copy-start | bytes 6148
  21.1 32.6 %copy-start.40 = (s32[5]{0:T(128)S(1)}, s32[5]{0:T(128)}, u32[]{:S(2)}) copy-start(s32[5]{0:T(128)} %constant.102) | copy-start | bytes 64
  21.1 33.8 %copy-start.38 = (s32[4]{0:T(128)S(1)}, s32[4]{0:T(128)}, u32[]{:S(2)}) copy-start(s32[4]{0:T(128)} %constant.104) | copy-start | bytes 52
  21.1 33.8 %copy-start.39 = (s32[4]{0:T(128)S(1)}, s32[4]{0:T(128)}, u32[]{:S(2)}) copy-start(s32[4]{0:T(128)} %constant.103) | copy-start | bytes 52
  21.1 34.5 %copy-start.14 = (bf16[640,640]{1,0:T(8,128)(2,1)S(1)}, bf16[640,640]{1,0:T(8,128)(2,1)}, u32[]{:S(2)}) copy-start(bf16[640,640]{1,0:T(8,128)(2,1)} %param.22) | copy-start | bytes 2457604
  21.1 191.8 %all-reduce.11.cloned.1.call-start = ((), (), s32[]{:S(2)}) async-start(), calls=%async_computation.1 | async-start | bytes 2097152 | tf_op jit(solution)/shard_map/psum | solution.py:16
  22.6 34.3 %copy-start.36 = (s32[3]{0:T(128)S(1)}, s32[3]{0:T(128)}, u32[]{:S(2)}) copy-start(s32[3]{0:T(128)} %constant.106) | copy-start | bytes 40
  22.6 34.3 %copy-start.37 = (s32[3]{0:T(128)S(1)}, s32[3]{0:T(128)}, u32[]{:S(2)}) copy-start(s32[3]{0:T(128)} %constant.105) | copy-start | bytes 40
  24.0 249.0 %all-reduce.13.cloned.1.call-start = ((), (), s32[]{:S(2)}) async-start(), calls=%async_computation.2 | async-start | bytes 2097152 | tf_op jit(solution)/shard_map/psum | solution.py:16
  24.3 39.4 %copy-start.33 = (f32[512]{0:T(512)}, f32[512]{0:T(512)S(1)}, u32[]{:S(2)}) copy-start(f32[512]{0:T(512)S(1)} %exponential_multiply_fusion) | copy-start | bytes 6148
  51.9 102.0 %copy-start.20 = (f32[1024]{0:T(1024)}, f32[1024]{0:T(1024)S(1)}, u32[]{:S(2)}) copy-start(f32[1024]{0:T(1024)S(1)} %get-tuple-element.34) | copy-start | bytes 12292
  54.3 4.9 %collective-permute-start.3 = (bf16[3,1,1,8,25,128]{5,4,3,2,1,0:T(8,128)(2,1)S(1)}, bf16[3,1,1,8,25,128]{5,4,3,2,1,0:T(8,128)(2,1)S(1)}, u32[]{:S(2)}, u32[]{:S(2)}) collective-permute-start(bf16[3,1,1,8,25,128]{5,4,3,2,1,0:T(8,128)(2,1)S(1)} %pad_maximum_fusion.3), channel_id=1, source_target_pairs={{2,0},{4,2},{6,4},{0,6},{3,1},{5,3},{7,5},{1,7},{10,8},{12,10},{14... | collective-permute-start | bytes 460808 | tf_op jit(solution)/shard_map/ppermute | solution.py:32
  54.4 8.1 %collective-permute-start.2 = (bf16[3,1,1,8,25,128]{5,4,3,2,1,0:T(8,128)(2,1)S(1)}, bf16[3,1,1,8,25,128]{5,4,3,2,1,0:T(8,128)(2,1)}, u32[]{:S(2)}, u32[]{:S(2)}) collective-permute-start(bf16[3,1,1,8,25,128]{5,4,3,2,1,0:T(8,128)(2,1)S(1)} %pad_maximum_fusion.3), channel_id=1, source_target_pairs={{0,2},{2,4},{4,6},{6,0},{1,3},{3,5},{5,7},{7,1},{8,10},{10,12},{12... | collective-permute-start | bytes 460808 | tf_op jit(solution)/shard_map/ppermute | solution.py:29
  55.6 98.3 %copy-start.1 = (f32[1024,128]{1,0:T(8,128)S(1)}, f32[1024,128]{1,0:T(8,128)}, u32[]{:S(2)}) copy-start(f32[1024,128]{1,0:T(8,128)} %param.26) | copy-start | bytes 1572868
  63.6 149.3 %collective-permute-start.5 = (bf16[3,3,1,8,25,128]{5,3,4,2,1,0:T(8,128)(2,1)S(1)}, bf16[3,3,1,8,25,128]{5,3,4,2,1,0:T(8,128)(2,1)}, u32[]{:S(2)}, u32[]{:S(2)}) collective-permute-start(bf16[3,3,1,8,25,128]{5,3,4,2,1,0:T(8,128)(2,1)S(1)} %copy.50), channel_id=1, source_target_pairs={{1,0},{0,1},{3,2},{2,3},{5,4},{4,5},{7,6},{6,7},{9,8},{8,9},{11,10... | collective-permute-start | bytes 1382408 | tf_op jit(solution)/shard_map/ppermute | solution.py:32
  64.1 150.0 %collective-permute-start.4 = (bf16[3,3,1,8,25,128]{5,3,4,2,1,0:T(8,128)(2,1)S(1)}, bf16[3,3,1,8,25,128]{5,3,4,2,1,0:T(8,128)(2,1)S(1)}, u32[]{:S(2)}, u32[]{:S(2)}) collective-permute-start(bf16[3,3,1,8,25,128]{5,3,4,2,1,0:T(8,128)(2,1)S(1)} %copy.50), channel_id=1, source_target_pairs={{0,1},{1,0},{2,3},{3,2},{4,5},{5,4},{6,7},{7,6},{8,9},{9,8},{10,11... | collective-permute-start | bytes 1382408 | tf_op jit(solution)/shard_map/ppermute | solution.py:29
  153.9 2.9 %copy-start.4 = (f32[1024,128]{1,0:T(8,128)S(1)}, f32[1024,128]{1,0:T(8,128)}, u32[]{:S(2)}) copy-start(f32[1024,128]{1,0:T(8,128)} %get-tuple-element.26) | copy-start | bytes 1572868
  153.9 3.4 %copy-start.2 = (f32[1024,128]{1,0:T(8,128)S(1)}, f32[1024,128]{1,0:T(8,128)}, u32[]{:S(2)}) copy-start(f32[1024,128]{1,0:T(8,128)} %get-tuple-element.27) | copy-start | bytes 1572868
  240.2 3.8 %copy-start.34 = (f32[512]{0:T(512)S(1)}, f32[512]{0:T(512)}, u32[]{:S(2)}) copy-start(f32[512]{0:T(512)} %copy-done.33) | copy-start | bytes 6148
  244.0 2.8 copy-start.10
  248.3 2.4 copy-start.30
  248.3 2.4 copy-start.31
  254.2 2.8 copy-start.24
  254.2 2.8 copy-start.25
  255.6 5.2 %copy-start.28 = (f32[512]{0:T(512)S(1)}, f32[512]{0:T(512)}, u32[]{:S(2)}) copy-start(f32[512]{0:T(512)} %get-tuple-element.71) | copy-start | bytes 6148
  255.6 5.2 %copy-start.29 = (f32[512]{0:T(512)S(1)}, f32[512]{0:T(512)}, u32[]{:S(2)}) copy-start(f32[512]{0:T(512)} %get-tuple-element.72) | copy-start | bytes 6148
  257.0 3.9 %copy-start.6 = (f32[512,4,128]{0,2,1:T(8,128)S(1)}, f32[512,4,128]{0,2,1:T(8,128)}, u32[]{:S(2)}) copy-start(f32[512,4,128]{0,2,1:T(8,128)} %copy.61) | copy-start | bytes 3145732
  257.0 3.9 %copy-start.7 = (f32[512,4,128]{0,2,1:T(8,128)S(1)}, f32[512,4,128]{0,2,1:T(8,128)}, u32[]{:S(2)}) copy-start(f32[512,4,128]{0,2,1:T(8,128)} %copy.63) | copy-start | bytes 3145732
  264.3 4.2 %copy-start.22 = (f32[16,32]{1,0:T(8,128)S(1)}, f32[16,32]{1,0:T(8,128)}, u32[]{:S(2)}) copy-start(f32[16,32]{1,0:T(8,128)} %get-tuple-element.66) | copy-start | bytes 6148
  264.3 4.2 %copy-start.23 = (f32[16,32]{1,0:T(8,128)S(1)}, f32[16,32]{1,0:T(8,128)}, u32[]{:S(2)}) copy-start(f32[16,32]{1,0:T(8,128)} %get-tuple-element.67) | copy-start | bytes 6148
  265.9 6.1 %copy-start.17 = (f32[1,1,1,16,25,128]{5,3,4,2,1,0:T(8,128)S(1)}, f32[1,1,1,16,25,128]{5,3,4,2,1,0:T(8,128)}, u32[]{:S(2)}) copy-start(f32[1,1,1,16,25,128]{5,3,4,2,1,0:T(8,128)} %constant_dynamic-update-slice_fusion.22) | copy-start | bytes 614404
  265.9 6.4 %copy-start.16 = (bf16[1,1,1,16,25,128]{5,3,4,2,1,0:T(8,128)(2,1)S(1)}, bf16[1,1,1,16,25,128]{5,3,4,2,1,0:T(8,128)(2,1)}, u32[]{:S(2)}) copy-start(bf16[1,1,1,16,25,128]{5,3,4,2,1,0:T(8,128)(2,1)} %param.17) | copy-start | bytes 307204
  268.5 4.4 %copy-start.21 = (f32[1024]{0:T(1024)S(1)}, f32[1024]{0:T(1024)}, u32[]{:S(2)}) copy-start(f32[1024]{0:T(1024)} %copy-done.20) | copy-start | bytes 12292
  268.5 4.4 %copy-start.26 = (f32[128]{0:T(128)S(1)}, f32[128]{0:T(128)}, u32[]{:S(2)}) copy-start(f32[128]{0:T(128)} %broadcast_multiply_fusion) | copy-start | bytes 1540
  268.5 6.0 %copy-start.18 = (f32[1,1,1,16,128]{4,3,2,1,0:T(8,128)S(1)}, f32[1,1,1,16,128]{4,3,2,1,0:T(8,128)}, u32[]{:S(2)}) copy-start(f32[1,1,1,16,128]{4,3,2,1,0:T(8,128)} %param.27) | copy-start | bytes 24580
  272.3 4.8 %copy-start.9 = (f32[16,1024]{1,0:T(8,128)S(1)}, f32[16,1024]{1,0:T(8,128)}, u32[]{:S(2)}) copy-start(f32[16,1024]{1,0:T(8,128)} %copy-done.8) | copy-start | bytes 196612
  273.0 3.4 %copy-start.11 = (f32[1024,128]{1,0:T(8,128)S(1)}, f32[1024,128]{1,0:T(8,128)}, u32[]{:S(2)}) copy-start(f32[1024,128]{1,0:T(8,128)} %get-tuple-element.37) | copy-start | bytes 1572868
  274.6 3.6 %copy-start.5 = (f32[1024,128]{1,0:T(8,128)S(1)}, f32[1024,128]{1,0:T(8,128)}, u32[]{:S(2)}) copy-start(f32[1024,128]{1,0:T(8,128)} %get-tuple-element.26) | copy-start | bytes 1572868
  276.4 2.4 copy-start.3
  277.1 2.3 copy-start.19
  277.1 2.3 copy-start.35
  (2 other events, 2.7 us)
Sparse Core Ops, SparseCore 0:
  21.2 132.6 all-reduce.8
  157.1 55.7 all-reduce.10
  215.4 51.2 all-reduce.12
